TPU v7x, 512 devices: a whole 4x8x8 slice. The times are simulated.
512 devices in a mesh: dp: 32 (over x, y_hi, core), fsdp: 16 (over y_lo, z).
Axes of the slice: x: 4, y: 8 (y_hi: 4, y_lo: 2; y = y_hi * 2 + y_lo), z: 8, core: 2. Of those that a mesh axis runs over, the one named last changes fastest.
Arguments:
- hidden: bfloat16 [4, 2048, 16, 4096], P(None, 'dp', 'fsdp'), may hold values from -6 to 6
- frozen_query_rows: bfloat16 [4, 2048, 16, 2048], P(None, 'dp', 'fsdp'), may hold values from -10 to 10
- output_gradient: bfloat16 [4, 2048, 16, 2048], P(None, 'dp', 'fsdp'), may hold values from -6 to 6
- token_log_ratio: float32 [4, 2048, 16], P(None, 'dp', 'fsdp'), may hold values from -0.15625 to 0.15625
- lengths: int32 [4], replicated, may hold values from 1 to 32768, as said below
- response_win_probability: float32 [4], replicated, may hold values from 0.05 to 0.95
- cached_prompt_keys: bfloat16 [1024, 512], P('fsdp'), may hold values from -7.5 to 7.5
- cached_prompt_values: bfloat16 [1024, 512], P('fsdp'), may hold values from -6 to 6
- adapter_down_factor: bfloat16 [4096, 64], P('fsdp'), may hold values from -0.09375 to 0.09375
- adapter_up_factor: bfloat16 [64, 2048], P(None, 'fsdp'), may hold values from -0.125 to 0.125
- attention_norm_gain: bfloat16 [4096], P('fsdp'), may hold values from 0.5 to 1.5
Outputs:
- grad_down: float32 [4096, 64], P('fsdp')
- grad_up: float32 [64, 2048], P(None, 'fsdp')
- seq_ratio: float32 [4], replicated
Inputs may be any that keep to these rules, and one draw needn't show every extreme that they name: The lengths sum to 65472 and the longest is exactly 32768.
All inputs are finite; a program needn't handle non-finite values.
Results may differ from a plain program's by a relative error of at most 0.012.
Values may be sent and summed in bfloat16 or wider, within the bound.
A program may use at most 128 MiB of HBM per device.

v0:
```python
import math
import jax
import jax.numpy as jnp
from jax import lax
from jax.sharding import PartitionSpec as P

HEAD_SIZE = 128
QUERY_HEADS = 16
KEY_VALUE_HEADS = 4
target_scale = 1.0
norm_epsilon = 1e-05


def attend(query_vectors, cotangent, key_rows, value_rows):
    row_count = query_vectors.shape[0]
    queries_per_group = QUERY_HEADS // KEY_VALUE_HEADS
    score_scale = 1.0 / math.sqrt(HEAD_SIZE)
    pieces = []
    for shared_key_head in range(KEY_VALUE_HEADS):
        head_start = shared_key_head * queries_per_group * HEAD_SIZE
        head_stop = head_start + queries_per_group * HEAD_SIZE
        head_query = query_vectors[:, head_start:head_stop].reshape(
            row_count, queries_per_group, HEAD_SIZE
        )
        head_grad = cotangent[:, head_start:head_stop].reshape(
            row_count, queries_per_group, HEAD_SIZE
        )
        head_key = key_rows[:, shared_key_head * HEAD_SIZE : (shared_key_head + 1) * HEAD_SIZE]
        head_value = value_rows[:, shared_key_head * HEAD_SIZE : (shared_key_head + 1) * HEAD_SIZE]
        scores = (
            jnp.einsum("nhd,jd->nhj", head_query, head_key, preferred_element_type=jnp.float32)
            * score_scale
        )
        row_top = jnp.max(scores, axis=2, keepdims=True)
        exponent = jnp.exp(scores - row_top)
        row_total = jnp.sum(exponent, axis=2, keepdims=True)
        weights = exponent.astype(jnp.bfloat16)
        mixed_out = (
            jnp.einsum("nhj,jd->nhd", weights, head_value, preferred_element_type=jnp.float32)
            / row_total
        )
        inner_prod = jnp.sum(head_grad.astype(jnp.float32) * mixed_out, axis=2, keepdims=True)
        grad_prob = jnp.einsum(
            "nhd,jd->nhj", head_grad, head_value, preferred_element_type=jnp.float32
        )
        grad_score = (weights.astype(jnp.float32) / row_total * (grad_prob - inner_prod)).astype(
            jnp.bfloat16
        )
        query_gradient = (
            jnp.einsum("nhj,jd->nhd", grad_score, head_key, preferred_element_type=jnp.float32)
            * score_scale
        )
        pieces.append(query_gradient.reshape(row_count, queries_per_group * HEAD_SIZE))
    return jnp.concatenate(pieces, axis=1).astype(jnp.bfloat16)


def body(
    hidden,
    frozen_query_rows,
    output_gradient,
    token_log_ratio,
    lengths,
    response_win_probability,
    cached_prompt_keys,
    cached_prompt_values,
    adapter_down_factor,
    adapter_up_factor,
    attention_norm_gain,
):
    fsdp_count = lax.axis_size("fsdp")
    dp_index = lax.axis_index("dp")
    fsdp_index = lax.axis_index("fsdp")
    responses, per_device, single, feature_count = hidden.shape
    home_rows = responses * per_device
    local_rows = jnp.arange(per_device, dtype=jnp.int32)
    position = (dp_index * per_device + local_rows) * fsdp_count + fsdp_index
    is_valid = position[None, :] < lengths[:, None]
    partial_value = jnp.sum(jnp.where(is_valid, token_log_ratio[:, :, 0], 0.0), axis=1)
    seq_ratio = lax.psum(partial_value, ("dp", "fsdp"))
    weighting = 2.0 * (seq_ratio - target_scale * (response_win_probability - 0.5)) / responses
    down_full, up_full, gain_full = (
        lax.all_gather(adapter_down_factor, "fsdp", axis=0, tiled=True),
        lax.all_gather(adapter_up_factor, "fsdp", axis=1, tiled=True),
        lax.all_gather(attention_norm_gain, "fsdp", axis=0, tiled=True),
    )
    key_rows, value_rows = (
        lax.all_gather(cached_prompt_keys, "fsdp", axis=0, tiled=True),
        lax.all_gather(cached_prompt_values, "fsdp", axis=0, tiled=True),
    )
    widened = hidden.reshape(home_rows, feature_count).astype(jnp.float32)
    inverse = lax.rsqrt(jnp.mean(widened * widened, axis=1, keepdims=True) + norm_epsilon)
    normed_input = (widened * inverse * gain_full.astype(jnp.float32)).astype(jnp.bfloat16)
    lowrank_hidden = jnp.dot(normed_input, down_full, preferred_element_type=jnp.float32).astype(
        jnp.bfloat16
    )
    row_mask = is_valid.reshape(home_rows)
    row_coef = jnp.repeat(weighting, per_device)
    base_rows = frozen_query_rows.reshape(home_rows, -1)
    cotangent = jnp.where(
        row_mask[:, None],
        row_coef[:, None] * output_gradient.reshape(home_rows, -1).astype(jnp.float32),
        0.0,
    ).astype(jnp.bfloat16)
    query_vectors = (
        base_rows.astype(jnp.float32)
        + jnp.dot(lowrank_hidden, up_full, preferred_element_type=jnp.float32)
    ).astype(jnp.bfloat16)
    query_gradient = attend(query_vectors, cotangent, key_rows, value_rows)
    up_term = jnp.dot(lowrank_hidden.T, query_gradient, preferred_element_type=jnp.float32)
    gradient_lowrank = jnp.dot(
        query_gradient, up_full.T, preferred_element_type=jnp.float32
    ).astype(jnp.bfloat16)
    down_term = jnp.dot(normed_input.T, gradient_lowrank, preferred_element_type=jnp.float32)
    down_sum, up_sum = lax.psum((down_term, up_term), ("dp", "fsdp"))
    down_factor_part = adapter_down_factor.shape[0]
    up_factor_part = adapter_up_factor.shape[1]
    grad_down = lax.dynamic_slice_in_dim(
        down_sum, fsdp_index * down_factor_part, down_factor_part, 0
    )
    grad_up = lax.dynamic_slice_in_dim(up_sum, fsdp_index * up_factor_part, up_factor_part, 1)
    return (grad_down, grad_up, seq_ratio)


def solution(mesh):
    in_specs = (
        P(None, "dp", "fsdp", None),
        P(None, "dp", "fsdp", None),
        P(None, "dp", "fsdp", None),
        P(None, "dp", "fsdp"),
        P(),
        P(),
        P("fsdp", None),
        P("fsdp", None),
        P("fsdp", None),
        P(None, "fsdp"),
        P("fsdp"),
    )
    out_specs = (P("fsdp", None), P(None, "fsdp"), P())
    return jax.shard_map(body, mesh=mesh, in_specs=in_specs, out_specs=out_specs, check_vma=False)
```

profile of v0, /device:TPU:17, one launch (start us, length us, event | category | flops | bytes accessed | tf_op | source)
XLA Modules:
  0.0 574.0 jit_solution(2248930495816452318)
XLA Ops:
  9.6 105.0 %psum.21 = f32[4]{0:T(128)S(1)} all-reduce(f32[4]{0:T(128)S(1)} %get-tuple-element.5), channel_id=1, replica_groups=mesh['dp'=32,'fsdp'=16] {'dp','fsdp'}, use_global_device_ids=true, to_apply=%region_4.5 | all-reduce | flops 4 | bytes 32 | tf_op jit(solution)/shard_map/psum | solution.py:79
  116.1 2.1 multiply_reduce_fusion
  118.3 24.8 %all-gather = bf16[16,1,256]{2,1,0:T(2,128)(2,1)S(1)} all-gather(bf16[1,1,256]{2,1,0:T(2,128)(2,1)S(1)} %reshape.122), channel_id=1, replica_groups=mesh['dp'=32,'fsdp'=16] {'fsdp'}, dimensions={0}, use_global_device_ids=true | all-gather | bytes 8704 | tf_op jit(solution)/shard_map/all_gather | solution.py:84
  143.1 2.2 fusion.1
  152.9 24.4 %all_gather.17 = bf16[64,2048]{1,0:T(8,128)(2,1)S(1)} all-gather(bf16[64,128]{1,0:T(8,128)(2,1)S(1)} %copy-done.17), channel_id=1, replica_groups=mesh['dp'=32,'fsdp'=16] {'fsdp'}, dimensions={1}, use_global_device_ids=true | all-gather | bytes 278528 | tf_op jit(solution)/shard_map/all_gather | solution.py:83
  177.3 27.5 %all_gather.16 = bf16[4096,64]{0,1:T(8,128)(2,1)S(1)} all-gather(bf16[256,64]{0,1:T(8,128)(2,1)S(1)} %copy-done.16), channel_id=1, replica_groups=mesh['dp'=32,'fsdp'=16] {'fsdp'}, dimensions={0}, use_global_device_ids=true | all-gather | bytes 557056 | tf_op jit(solution)/shard_map/all_gather | solution.py:82
  208.8 2.0 copy-done
  211.9 3.0 fusion.39
  216.4 1.9 multiply_reduce_fusion.1
  218.3 1.9 copy-done.1
  222.0 3.1 fusion.30
  226.6 1.8 multiply_reduce_fusion.2
  228.4 2.0 copy-done.2
  232.1 3.1 fusion.33
  236.6 1.8 multiply_reduce_fusion.3
  238.4 1.9 copy-done.3
  242.3 3.1 fusion.36
  246.9 4.8 fusion.21
  251.7 4.8 fusion.24
  256.5 4.8 fusion.23
  261.3 4.8 fusion.22
  266.2 3.6 fusion.25
  269.8 2.2 fusion.70
  272.0 292.6 %all-reduce.3.cloned.1.call-done = (f32[4096,64]{0,1:T(8,128)}, f32[64,2048]{1,0:T(8,128)}) async-done(((f32[4096,64]{0,1:T(8,128)}, f32[64,2048]{1,0:T(8,128)}), (f32[4096,64]{0,1:T(8,128)}, f32[64,2048]{1,0:T(8,128)})) %all-reduce.3.cloned.1.call-update) | async-done | bytes 1572880 | tf_op jit(solution)/shard_map/psum | solution.py:114
  (106 shorter events, 30.8 us)
Async XLA Ops:
  7.2 138.2 %copy-start.6 = (bf16[4,64,1,2048]{3,1,2,0:T(8,128)(2,1)S(1)}, bf16[4,64,1,2048]{3,1,2,0:T(8,128)(2,1)}, u32[]{:S(2)}) copy-start(bf16[4,64,1,2048]{3,1,2,0:T(8,128)(2,1)} %param.13) | copy-start | bytes 3145732
  7.2 199.9 %all-gather.4.cloned.1.call-start = ((), (), s32[]{:S(2)}) async-start(), calls=%async_computation | async-start | bytes 1114112 | tf_op jit(solution)/shard_map/all_gather | solution.py:87
  7.9 204.0 %all-gather.6.cloned.1.call-start = ((), (), s32[]{:S(2)}) async-start(), calls=%async_computation.1 | async-start | bytes 1114112 | tf_op jit(solution)/shard_map/all_gather | solution.py:88
  8.7 555.9 %all-reduce.3.cloned.1.call-start = ((), (), s32[]{:S(2)}) async-start(), calls=%async_computation.2 | async-start | bytes 3145728 | tf_op jit(solution)/shard_map/psum | solution.py:114
  114.6 3.7 copy-start.31
  145.3 7.6 %copy-start.17 = (bf16[64,128]{1,0:T(8,128)(2,1)S(1)}, bf16[64,128]{1,0:T(8,128)(2,1)}, u32[]{:S(2)}) copy-start(bf16[64,128]{1,0:T(8,128)(2,1)} %param.20) | copy-start | bytes 49156
  145.4 32.0 %copy-start.16 = (bf16[256,64]{0,1:T(8,128)(2,1)S(1)}, bf16[256,64]{0,1:T(8,128)(2,1)}, u32[]{:S(2)}) copy-start(bf16[256,64]{0,1:T(8,128)(2,1)} %param.19) | copy-start | bytes 98308
  145.7 59.9 %copy-start.5 = (bf16[4,64,1,2048]{3,1,2,0:T(8,128)(2,1)S(1)}, bf16[4,64,1,2048]{3,1,2,0:T(8,128)(2,1)}, u32[]{:S(2)}) copy-start(bf16[4,64,1,2048]{3,1,2,0:T(8,128)(2,1)} %param.12) | copy-start | bytes 3145732
  210.8 4.2 copy-start.10
  211.7 6.6 %copy-start.18 = (f32[256,4]{0,1:T(4,128)}, f32[256,4]{0,1:T(4,128)S(1)}, u32[]{:S(2)}) copy-start(f32[256,4]{0,1:T(4,128)S(1)} %fusion.2) | copy-start | bytes 12292
  216.4 5.6 copy-start.4
  222.0 3.1 copy-start.11
  232.1 3.1 copy-start.12
  242.3 3.1 copy-start.13
  246.9 4.8 copy-start.20
  246.9 4.8 copy-start.25
  251.7 4.8 copy-start.22
  251.7 4.8 copy-start.26
  256.5 4.8 copy-start.24
  256.5 4.8 copy-start.27
  266.2 3.7 copy-start.15
  266.2 3.7 copy-start.28
  266.2 3.7 copy-start.29
  266.2 3.7 copy-start.30
  (11 other events, 20.1 us)
Sparse Core Ops, SparseCore 0:
  10.1 66.9 all-gather.3
  79.2 69.6 all-gather.5
  272.2 292.3 all-reduce.2
where the time goes:
time: 575 us; the launch traced here: 574 us
  waiting for transfers between devices  294 us (51%)
  blocking collectives  182 us (32%)
  matrix products  45.8 us (8%)
  local copies, waits for them, and re-layouts  25.3 us (4%)
  between operations  14.1 us (2%)
  other arithmetic  13.1 us (2%)
    psum x1, waiting for transfers between devices, body(): down_sum, up_sum = lax.psum((down_term, up_term), ('dp', 'fsdp'))  293 us
    psum x1, blocking collectives, body(): seq_ratio = lax.psum(partial_value, ('dp', 'fsdp'))  105 us
    all_gather x1, blocking collectives, body(): lax.all_gather(adapter_down_factor, 'fsdp', axis=0, tiled=True)  27.5 us
    all_gather x1, blocking collectives, body(): lax.all_gather(attention_norm_gain, 'fsdp', axis=0, tiled=True)  24.8 us
    all_gather x1, blocking collectives, body(): lax.all_gather(adapter_up_factor, 'fsdp', axis=1, tiled=True)  24.4 us
    dot_general x4, matrix products, attend(): jnp.einsum('nhj,jd->nhd', grad_score, head_key, preferred_element_type=jn...  19.2 us
    dot_general x4, matrix products, attend(): jnp.einsum('nhj,jd->nhd', weights, head_value, preferred_element_type=jnp...  12.3 us
  transfers between devices with their start and end apart: 3, of which 1 were waited for; matrix products, arithmetic and copies ran while one was open for 3% of the time, Pallas kernels for 0%

commit v1 on v0

--- a/solution.py
+++ b/solution.py
@@ -76,7 +76,7 @@
     position = (dp_index * per_device + local_rows) * fsdp_count + fsdp_index
     is_valid = position[None, :] < lengths[:, None]
     partial_value = jnp.sum(jnp.where(is_valid, token_log_ratio[:, :, 0], 0.0), axis=1)
-    seq_ratio = lax.psum(partial_value, ("dp", "fsdp"))
+    seq_ratio = jnp.sum(lax.all_gather(partial_value, ("dp", "fsdp")), axis=0)
     weighting = 2.0 * (seq_ratio - target_scale * (response_win_probability - 0.5)) / responses
     down_full, up_full, gain_full = (
         lax.all_gather(adapter_down_factor, "fsdp", axis=0, tiled=True),

time: 575 us -> 551 us (0.958)
  blocking collectives: 182 us -> 203 us
  waiting for transfers between devices: 294 us -> 274 us
  local copies, waits for them, and re-layouts: 25.3 us -> 10 us
  other arithmetic: 13.1 us -> 7.15 us
    unnamed x0 -> x1, blocking collectives: none -> 116 us
    psum x1 -> x0, blocking collectives: 105 us -> none  [body(): seq_ratio = lax.psum(partial_value, ('dp', 'fsdp'))]
    psum x1, waiting for transfers between devices: 293 us -> 273 us  [body(): down_sum, up_sum = lax.psum((down_term, up_term), ('dp', 'fsdp'))]
    all_gather x1, blocking collectives: 24.8 us -> 32.6 us  [body(): lax.all_gather(attention_norm_gain, 'fsdp', axis=0, tiled=True)]
    reshape x4 -> x0, local copies, waits for them, and re-layouts: 5.92 us -> none  [attend(): cotangent[:, head_start:head_stop]]
where the time goes in v1:
time: 551 us
  waiting for transfers between devices  274 us (50%)
  blocking collectives  203 us (37%)
  matrix products  42.5 us (8%)
  between operations  14 us (3%)
  local copies, waits for them, and re-layouts  10 us (2%)
  other arithmetic  7.15 us (1%)
    psum x1, waiting for transfers between devices, body(): down_sum, up_sum = lax.psum((down_term, up_term), ('dp', 'fsdp'))  273 us
    unnamed x1, blocking collectives  116 us
    all_gather x1, blocking collectives, body(): lax.all_gather(attention_norm_gain, 'fsdp', axis=0, tiled=True)  32.6 us
    all_gather x1, blocking collectives, body(): lax.all_gather(adapter_down_factor, 'fsdp', axis=0, tiled=True)  27.4 us
    all_gather x1, blocking collectives, body(): lax.all_gather(adapter_up_factor, 'fsdp', axis=1, tiled=True)  26.9 us
    dot_general x4, matrix products, attend(): jnp.einsum('nhj,jd->nhd', grad_score, head_key, preferred_element_type=jn...  19.1 us
    dot_general x4, matrix products, attend(): jnp.einsum('nhj,jd->nhd', weights, head_value, preferred_element_type=jnp...  12.8 us
  transfers between devices with their start and end apart: 3, of which 1 were waited for; matrix products, arithmetic and copies ran while one was open for 3% of the time, Pallas kernels for 0%

profile of v1, /device:TPU:17, one launch (start us, length us, event | category | flops | bytes accessed | tf_op | source)
XLA Modules:
  0.0 550.9 jit_solution(14064353366586891318)
XLA Ops:
  9.4 32.6 %all-gather.1 = bf16[16,1,256]{2,1,0:T(2,128)(2,1)S(1)} all-gather(bf16[1,1,256]{2,1,0:T(2,128)(2,1)S(1)} %reshape.125), channel_id=1, replica_groups=mesh['dp'=32,'fsdp'=16] {'fsdp'}, dimensions={0}, use_global_device_ids=true | all-gather | bytes 8704 | tf_op jit(solution)/shard_map/all_gather | solution.py:84
  42.0 2.1 multiply_reduce_fusion
  44.2 27.4 %all_gather.22 = bf16[4096,64]{0,1:T(8,128)(2,1)S(1)} all-gather(bf16[256,64]{0,1:T(8,128)(2,1)} %param.19), channel_id=1, replica_groups=mesh['dp'=32,'fsdp'=16] {'fsdp'}, dimensions={0}, use_global_device_ids=true | all-gather | bytes 557056 | tf_op jit(solution)/shard_map/all_gather | solution.py:82
  71.6 26.9 %all_gather.23 = bf16[64,2048]{1,0:T(8,128)(2,1)S(1)} all-gather(bf16[64,128]{1,0:T(8,128)(2,1)} %param.20), channel_id=1, replica_groups=mesh['dp'=32,'fsdp'=16] {'fsdp'}, dimensions={1}, use_global_device_ids=true | all-gather | bytes 278528 | tf_op jit(solution)/shard_map/all_gather | solution.py:83
  99.2 1.3 copy-done.5
  102.4 116.1 %all-reduce = f32[2048]{0:T(1024)S(1)} all-reduce(f32[2048]{0:T(1024)S(1)} %dynamic-update-slice), channel_id=2, replica_groups=mesh['dp'=32,'fsdp'=16] {'dp','fsdp'}, use_global_device_ids=true, to_apply=%add | all-reduce | flops 2048 | bytes 16384
  220.2 1.8 multiply_reduce_fusion.4
  222.8 0.9 fusion.2
  226.1 0.9 fusion.6
  227.0 1.0 copy-done.2
  228.8 1.9 copy-done
  231.7 3.2 fusion.29
  234.9 4.8 fusion.25
  239.7 3.2 fusion.30
  243.0 4.4 fusion.26
  247.3 3.2 fusion.31
  250.5 4.8 fusion.27
  255.4 3.2 fusion.32
  258.6 5.0 fusion.28
  263.6 2.3 fusion.54
  265.9 3.0 fusion.33
  268.9 272.6 %all-reduce.4.cloned.1.call-done = (f32[4096,64]{0,1:T(8,128)}, f32[64,2048]{1,0:T(8,128)}) async-done(((f32[4096,64]{0,1:T(8,128)}, f32[64,2048]{1,0:T(8,128)}), (f32[4096,64]{0,1:T(8,128)}, f32[64,2048]{1,0:T(8,128)})) %all-reduce.4.cloned.1.call-update) | async-done | bytes 1572880 | tf_op jit(solution)/shard_map/psum | solution.py:114
  541.5 1.5 constant_dynamic-slice_fusion.1
  543.0 1.4 constant_dynamic-slice_fusion
  (64 shorter events, 11.2 us)
Async XLA Ops:
  7.2 91.3 %copy-start.4 = (bf16[4,64,1,4096]{3,1,2,0:T(8,128)(2,1)S(1)}, bf16[4,64,1,4096]{3,1,2,0:T(8,128)(2,1)}, u32[]{:S(2)}) copy-start(bf16[4,64,1,4096]{3,1,2,0:T(8,128)(2,1)} %param.11) | copy-start | bytes 6291460
  7.2 213.0 %all-gather.5.cloned.1.call-start = ((), (), s32[]{:S(2)}) async-start(), calls=%async_computation | async-start | bytes 1114112 | tf_op jit(solution)/shard_map/all_gather | solution.py:87
  7.9 223.8 %all-gather.7.cloned.1.call-start = ((), (), s32[]{:S(2)}) async-start(), calls=%async_computation.1 | async-start | bytes 1114112 | tf_op jit(solution)/shard_map/all_gather | solution.py:88
  8.7 532.8 %all-reduce.4.cloned.1.call-start = ((), (), s32[]{:S(2)}) async-start(), calls=%async_computation.2 | async-start | bytes 3145728 | tf_op jit(solution)/shard_map/psum | solution.py:114
  44.1 57.2 %copy-start.7 = (bf16[4,64,1,2048]{3,1,2,0:T(8,128)(2,1)S(1)}, bf16[4,64,1,2048]{3,1,2,0:T(8,128)(2,1)}, u32[]{:S(2)}) copy-start(bf16[4,64,1,2048]{3,1,2,0:T(8,128)(2,1)} %param.12) | copy-start | bytes 3145732
  99.2 1.4 copy-start.5
  100.6 1.4 copy-start.10
  100.6 1.4 copy-start.12
  100.6 118.3 %copy-start.13 = (f32[4]{0:T(128)S(1)}, f32[4]{0:T(128)}, u32[]{:S(2)}) copy-start(f32[4]{0:T(128)} %param.16) | copy-start | bytes 52
  100.6 118.6 %copy-start.8 = (bf16[4,64,1,2048]{3,1,2,0:T(8,128)(2,1)S(1)}, bf16[4,64,1,2048]{3,1,2,0:T(8,128)(2,1)}, u32[]{:S(2)}) copy-start(bf16[4,64,1,2048]{3,1,2,0:T(8,128)(2,1)} %param.13) | copy-start | bytes 3145732
  218.9 3.1 copy-start.11
  220.1 1.9 copy-start.9
  222.0 2.0 copy-start.3
  222.8 2.5 copy-start.1
  226.1 2.0 copy-start.2
  228.8 1.9 copy-start
  258.6 5.0 copy-start.14
  258.6 7.3 %copy-start.6 = (bf16[256,4096]{1,0:T(8,128)(2,1)S(1)}, bf16[256,4096]{1,0:T(8,128)(2,1)}, u32[]{:S(2)}) copy-start(bf16[256,4096]{1,0:T(8,128)(2,1)} %copy-done.5) | copy-start | bytes 6291460
Sparse Core Ops, SparseCore 0:
  10.1 67.6 all-gather.4
  79.9 69.0 all-gather.6
  269.0 272.4 all-reduce.3
